TPU v7x, 32 devices: a whole 2x2x4 slice. The times are simulated.
32 devices in a mesh: groups: 2 (over y), seq: 4 (over z), head: 2 (over x), sub: 2 (over core).
Axes of the slice: x: 2, y: 2, z: 4, core: 2. Of those that a mesh axis runs over, the one named last changes fastest.
Arguments:
- queries: bfloat16 [4608, 8192], P(('groups', 'seq'), ('head', 'sub')), parts along dimension 0, may hold values from -6 to 6
- keys: bfloat16 [4608, 8192], P(('groups', 'seq'), ('head', 'sub')), parts along dimension 0, may hold values from -0.0546875 to 0.0546875
- values: bfloat16 [4608, 8192], P(('groups', 'seq'), ('head', 'sub')), parts along dimension 0, may hold values from -800 to 800
- decay_exp: int32 [64], P(('head', 'sub')), may hold values from 1 to 2303, as said below
- gain: float32 [8192], P(('head', 'sub')), may hold values from 0.5 to 1.5
Outputs:
- normed: bfloat16 [4608, 8192], P(('groups', 'seq'), ('head', 'sub')), parts along dimension 0
- final_state: float32 [128, 128, 128], P(('groups', 'head', 'sub'), 'seq'), parts along dimension 0
There are 2 independent parts, one for each index of `groups`. A program takes and returns all parts, laid end to end along the dimension named above; an argument that names none is the same for every part. Nothing has to cross between parts.
Inputs may be any that keep to these rules, and one draw needn't show every extreme that they name: The decay of head h over one position is 2 ** (-decay_exp[h] / 18432).
All inputs are finite; a program needn't handle non-finite values.
Results may differ from a plain program's by a relative error of at most 0.0049.
Values sent between devices are 32-bit elements; how exact they have to be, the bound alone decides.
A program may use at most 64 MiB of HBM per device.

v0:
```python
import jax
import jax.numpy as jnp
from jax import lax
from jax.sharding import PartitionSpec as P

HEADS = 64
DK = 128


def local(queries, keys, values, decay_exp, gain):
    tokens = queries.shape[0]
    heads_here = decay_exp.shape[0]
    head_size = queries.shape[1] // heads_here
    n_seq = lax.axis_size("seq")
    decay_rate = decay_exp.astype(jnp.float32) / (8.0 * tokens * n_seq)
    offsets = jnp.arange(tokens).astype(jnp.float32)
    distance = offsets[:, None] - offsets[None, :]
    causal = distance >= 0
    within = jnp.where(
        causal[None], jnp.exp2(-decay_rate[:, None, None] * jnp.maximum(distance, 0.0)[None]), 0.0
    )
    key_decay = jnp.exp2(-decay_rate[None, :] * (tokens - 1.0 - offsets)[:, None])
    query_decay = jnp.exp2(-decay_rate[None, :] * (offsets + 1.0)[:, None])
    query_heads = queries.reshape(tokens, heads_here, head_size)
    key_heads = keys.reshape(tokens, heads_here, head_size)
    value_heads = values.reshape(tokens, heads_here, head_size)
    scaled_keys = (key_heads.astype(jnp.float32) * key_decay[:, :, None]).astype(jnp.bfloat16)
    local_state = jnp.einsum(
        "ihd,ihe->hde", scaled_keys, value_heads, preferred_element_type=jnp.float32
    )
    row_pieces = lax.all_to_all(local_state[None], "seq", split_axis=2, concat_axis=0, tiled=True)
    ranks = jnp.arange(n_seq).astype(jnp.float32)
    gap = ranks[:, None] - 1.0 - ranks[None, :]
    prior = jnp.where(
        gap[:, :, None] >= 0,
        jnp.exp2(-decay_rate[None, None, :] * tokens * jnp.maximum(gap, 0.0)[:, :, None]),
        0.0,
    )
    toward_end = jnp.exp2(-decay_rate[None, :] * tokens * (n_seq - 1.0 - ranks)[:, None])
    prefix_by_block = jnp.einsum(
        "bmh,mhre->bhre", prior, row_pieces, precision=lax.Precision.HIGHEST
    )
    final_rows = jnp.einsum("mh,mhre->hre", toward_end, row_pieces, precision=lax.Precision.HIGHEST)
    prefix = lax.all_to_all(prefix_by_block, "seq", split_axis=0, concat_axis=2, tiled=True)[0]
    scores = jnp.einsum("ihd,jhd->hij", query_heads, key_heads, preferred_element_type=jnp.float32)
    weights = (scores * within).astype(jnp.bfloat16)
    intra = jnp.einsum("hij,jhd->ihd", weights, value_heads, preferred_element_type=jnp.float32)
    decayed_query = query_heads.astype(jnp.float32) * query_decay[:, :, None]
    inter = jnp.einsum("ihd,hde->ihe", decayed_query, prefix, precision=lax.Precision.HIGHEST)
    mixed = (intra + inter).reshape(tokens, heads_here * head_size)
    squares = jnp.sum(mixed * mixed, axis=1)
    summed = lax.psum(squares, ("head", "sub"))
    mean_square = summed / (HEADS * DK)
    normed = (mixed * lax.rsqrt(mean_square + 1e-06)[:, None] * gain[None, :]).astype(jnp.bfloat16)
    return (normed, final_rows)


def solution(mesh):
    return jax.shard_map(
        local,
        mesh=mesh,
        in_specs=(
            P(("groups", "seq"), ("head", "sub")),
            P(("groups", "seq"), ("head", "sub")),
            P(("groups", "seq"), ("head", "sub")),
            P(("head", "sub")),
            P(("head", "sub")),
        ),
        out_specs=(
            P(("groups", "seq"), ("head", "sub")),
            P(("groups", "head", "sub"), "seq", None),
        ),
        check_vma=False,
    )
```

profile of v0, /device:TPU:0, one launch (start us, length us, event | category | flops | bytes accessed | tf_op | source)
XLA Modules:
  0.0 92.8 jit_solution(15200276459177829985)
XLA Ops:
  0.6 0.0 copy-start
  0.7 0.8 broadcast_multiply_fusion
  1.5 0.1 multiply_exponential_fusion
  1.6 4.7 %fusion.30 = f32[1,16,128,128]{3,2,1,0:T(8,128)S(1)} fusion(f32[576,16]{0,1:T(8,128)S(1)} %get-tuple-element.3, bf16[576,2048]{1,0:T(8,128)(2,1)} %param.7, bf16[576,2048]{1,0:T(8,128)(2,1)} %param.6), kind=kOutput, calls=%fused_computation.30 | convolution fusion | flops 305528832 | bytes 5804032 | tf_op jit(solution)/shard_map/ihd,ihe->hde/dot_general | solution.py:28
  6.3 1.6 %copy.34 = f32[1,16,128,128]{3,1,0,2:T(8,128)} copy(f32[1,16,128,128]{3,2,1,0:T(8,128)S(1)} %fusion.30) | data formatting | bytes 2097152 | tf_op jit(solution)/shard_map/broadcast_in_dim | solution.py:31
  7.8 6.3 %all-to-all-start = ((f32[1,16,128,128]{3,1,0,2:T(8,128)}), f32[1,16,128,128]{3,1,0,2:T(8,128)S(1)}, u32[]{:S(2)}, u32[]{:S(2)}) async-start(f32[1,16,128,128]{3,1,0,2:T(8,128)} %copy.34), calls=%async_computation | async-start | bytes 2097152 | tf_op jit(solution)/shard_map/all_to_all | solution.py:31
  14.2 0.1 exponential_bitcast_fusion
  14.3 0.1 copy.42
  14.4 0.1 subtract_compare_fusion.1
  14.4 0.1 subtract_maximum_fusion.1
  14.5 1.1 %subtract_compare_fusion = pred[576,576]{1,0:T(8,128)(4,1)} fusion(f32[576]{0:T(1024)S(1)} %iota_convert_fusion), kind=kLoop, calls=%fused_computation.23 | loop fusion | flops 663552 | bytes 334080 | tf_op jit(solution)/shard_map/ge | solution.py:18
  15.6 1.3 %subtract_maximum_fusion = f32[576,576]{1,0:T(8,128)} fusion(f32[576]{0:T(1024)S(1)} %iota_convert_fusion), kind=kLoop, calls=%fused_computation.22 | loop fusion | flops 663552 | bytes 1329408 | tf_op jit(solution)/shard_map/max | solution.py:20
  16.9 23.1 %all-to-all-done = f32[1,16,128,128]{3,1,0,2:T(8,128)S(1)} async-done(((f32[1,16,128,128]{3,1,0,2:T(8,128)}), f32[1,16,128,128]{3,1,0,2:T(8,128)S(1)}, u32[]{:S(2)}, u32[]{:S(2)}) %all-to-all-start) | async-done | bytes 1048608 | tf_op jit(solution)/shard_map/all_to_all | solution.py:31
  39.9 2.5 %convolution_bitcast_fusion = f32[4,16,32,128]{3,0,2,1:T(4,128)S(1)} fusion(f32[1,16,4,32,128]{4,1,3,2,0:T(8,128)S(1)} %bitcast.93, f32[4,4]{1,0:T(4,128)S(1)} %subtract_maximum_fusion.1, f32[16]{0:T(128)S(1)} %get-tuple-element.4, pred[4,4]{1,0:T(4,128)(4,1)S(1)} %subtract_compare_fusion.1), kind=kOutput, calls=%fused_computation.31 | convolution fusion | flops 12583680 | bytes 2097296 | tf_op jit(solution)/shard_map/bmh,mhre->bhre/dot_general | solution.py:40
  42.4 1.1 %copy.37 = f32[4,16,32,128]{3,2,1,0:T(8,128)} copy(f32[4,16,32,128]{3,0,2,1:T(4,128)S(1)} %convolution_bitcast_fusion) | data formatting | bytes 2097152 | tf_op jit(solution)/shard_map/bmh,mhre->bhre/transpose | solution.py:40
  43.6 4.4 %all-to-all-start.1 = ((f32[4,16,32,128]{3,2,1,0:T(8,128)}), f32[4,16,32,128]{3,2,1,0:T(8,128)}, u32[]{:S(2)}, u32[]{:S(2)}) async-start(f32[4,16,32,128]{3,2,1,0:T(8,128)} %copy.37), calls=%async_computation.1 | async-start | bytes 2097152 | tf_op jit(solution)/shard_map/all_to_all | solution.py:44
  48.0 0.0 copy-done
  48.1 12.4 %fusion = f32[16,576,128]{2,1,0:T(8,128)} fusion(f32[576,576]{1,0:T(8,128)} %subtract_maximum_fusion, f32[16]{0:T(128)S(1)} %get-tuple-element.5, pred[576,576]{1,0:T(8,128)(4,1)} %subtract_compare_fusion, bf16[576,2048]{1,0:T(8,128)(2,1)} %param.7, bf16[576,2048]{1,0:T(8,128)(2,1)} %param.6, bf16[576,2048]{1,0:T(8,128)(2,1)S(1)} %copy-done), kind=kOutput, calls=%fused_computation.1 | convolution fusion | flops 2744451072 | bytes 13455424 | tf_op jit(solution)/shard_map/hij,jhd->ihd/dot_general | solution.py:47
  60.5 3.1 %fusion.33 = f32[16,1,32,128]{3,1,2,0:T(1,128)} fusion(f32[4,16,1,1]{0,2,3,1:T(1,128)S(1)} %copy.42, f32[1,16,4,32,128]{4,1,3,2,0:T(8,128)S(1)} %bitcast.94), kind=kOutput, calls=%fused_computation.32 | convolution fusion | flops 3145728 | bytes 1310976 | tf_op jit(solution)/shard_map/mh,mhre->hre/dot_general | solution.py:43
  63.6 9.6 %all-to-all-done.1 = f32[4,16,32,128]{3,2,1,0:T(8,128)} async-done(((f32[4,16,32,128]{3,2,1,0:T(8,128)}), f32[4,16,32,128]{3,2,1,0:T(8,128)}, u32[]{:S(2)}, u32[]{:S(2)}) %all-to-all-start.1) | async-done | bytes 1048608 | tf_op jit(solution)/shard_map/all_to_all | solution.py:44
  73.2 1.3 %copy.38 = f32[4,16,32,128]{3,2,0,1:T(8,128)S(1)} copy(f32[4,16,32,128]{3,2,1,0:T(8,128)} %all-to-all-done.1) | data formatting | bytes 2097152 | tf_op jit(solution)/shard_map/all_to_all | solution.py:44
  74.5 0.0 copy-start.1
  74.5 8.2 %multiply_reduce_fusion = (f32[576]{0:T(1024)S(1)}, f32[576,16,128]{2,0,1:T(8,128)}) fusion(f32[16,128,128]{2,1,0:T(8,128)S(1)} %bitcast.95, f32[576,16]{0,1:T(8,128)S(1)} %get-tuple-element.2, f32[16,576,128]{2,1,0:T(8,128)} %fusion, bf16[576,2048]{1,0:T(8,128)(2,1)S(1)} %copy-done), kind=kOutput, calls=%fused_computation.8 | convolution fusion | flops 1817837056 | bytes 12884224 | tf_op jit(solution)/shard_map/ihd,hde->ihe/dot_general | solution.py:49
  82.7 5.8 %psum.7 = f32[576]{0:T(1024)S(1)} all-reduce(f32[576]{0:T(1024)S(1)} %get-tuple-element.6), channel_id=1, replica_groups=mesh['groups'=2,'seq'=4,'head'=2,'sub'=2] {'head','sub'}, use_global_device_ids=true, to_apply=%region_1.2 | all-reduce | flops 576 | bytes 4608 | tf_op jit(solution)/shard_map/psum | solution.py:52
  88.6 0.0 copy-done.1
  88.6 4.2 %fusion.5 = bf16[576,2048]{1,0:T(8,128)(2,1)} fusion(f32[2048]{0:T(1024)S(1)} %copy-done.1, f32[576]{0:T(1024)S(1)} %add_rsqrt_fusion, f32[576,16,128]{2,0,1:T(8,128)} %get-tuple-element.7), kind=kLoop, calls=%fused_computation.6 | loop fusion | flops 3538944 | bytes 7088384 | tf_op jit(solution)/shard_map/convert_element_type | solution.py:54
  (6 shorter events, 0.0 us)
Async XLA Ops:
  0.6 47.4 %copy-start = (bf16[576,2048]{1,0:T(8,128)(2,1)S(1)}, bf16[576,2048]{1,0:T(8,128)(2,1)}, u32[]{:S(2)}) copy-start(bf16[576,2048]{1,0:T(8,128)(2,1)} %param.5) | copy-start | bytes 7077892
  7.8 32.1 %all-to-all-start = ((f32[1,16,128,128]{3,1,0,2:T(8,128)}), f32[1,16,128,128]{3,1,0,2:T(8,128)S(1)}, u32[]{:S(2)}, u32[]{:S(2)}) async-start(f32[1,16,128,128]{3,1,0,2:T(8,128)} %copy.34), calls=%async_computation | async-start | bytes 2097152 | tf_op jit(solution)/shard_map/all_to_all | solution.py:31
  43.6 29.6 %all-to-all-start.1 = ((f32[4,16,32,128]{3,2,1,0:T(8,128)}), f32[4,16,32,128]{3,2,1,0:T(8,128)}, u32[]{:S(2)}, u32[]{:S(2)}) async-start(f32[4,16,32,128]{3,2,1,0:T(8,128)} %copy.37), calls=%async_computation.1 | async-start | bytes 2097152 | tf_op jit(solution)/shard_map/all_to_all | solution.py:44
  74.5 14.1 %copy-start.1 = (f32[2048]{0:T(1024)S(1)}, f32[2048]{0:T(1024)}, u32[]{:S(2)}) copy-start(f32[2048]{0:T(1024)} %param.9) | copy-start | bytes 24580
where the time goes:
time: 93.2 us; the launch traced here: 92.8 us
  waiting for transfers between devices  32.7 us (35%)
  matrix products  31 us (33%)
  starting transfers between devices  10.8 us (12%)
  other arithmetic  7.7 us (8%)
  blocking collectives  5.83 us (6%)
  local copies, waits for them, and re-layouts  4.14 us (4%)
    all_to_all x1, waiting for transfers between devices, local(): lax.all_to_all(local_state[None], 'seq', split_axis=2, concat_axis=0, til...  23.1 us
    dot_general x1, matrix products, local(): jnp.einsum('hij,jhd->ihd', weights, value_heads, preferred_element_type=j...  12.4 us
    all_to_all x1, waiting for transfers between devices, local(): lax.all_to_all(prefix_by_block, 'seq', split_axis=0, concat_axis=2, tiled...  9.61 us
    dot_general x1, matrix products, local(): jnp.einsum('ihd,hde->ihe', decayed_query, prefix, precision=lax.Precision...  8.2 us
    all_to_all x1, starting transfers between devices, local(): lax.all_to_all(local_state[None], 'seq', split_axis=2, concat_axis=0, til...  6.35 us
    psum x1, blocking collectives, local(): summed = lax.psum(squares, ('head', 'sub'))  5.83 us
    dot_general x1, matrix products, local(): jnp.einsum('ihd,ihe->hde', scaled_keys, value_heads, preferred_element_ty...  4.7 us
    all_to_all x1, starting transfers between devices, local(): lax.all_to_all(prefix_by_block, 'seq', split_axis=0, concat_axis=2, tiled...  4.44 us
  transfers between devices with their start and end apart: 2, of which 2 were waited for; matrix products, arithmetic and copies ran while one was open for 20% of the time, Pallas kernels for 0%

commit v1 on v0

v1 whole, which is shorter than its diff:
```python
import functools

import jax
import jax.numpy as jnp
from jax import lax
from jax.experimental import pallas as pl
from jax.experimental.pallas import tpu as pltpu
from jax.sharding import PartitionSpec as P

MESH = pl.DeviceIdType.MESH
F32 = jnp.float32
BF16 = jnp.bfloat16
PIECES = 2
ROW_BLOCK = 192


def dot(a, b, dims):
    return lax.dot_general(a, b, (dims, ((), ())), preferred_element_type=F32)


def mix_kernel(
    n_seq, n_head, n_sub, heads, dk,
    exps, q_hbm, k_hbm, v_hbm,
    mixed_hbm, inv_hbm, final_hbm,
    q_buf, k_buf, v_buf, mix, held, outgoing, final_rows, squares, sums, inv,
    in_sem, out_sem, send_sem, recv_sem, fin_send, fin_recv, sum_send, sum_recv, tail_sem,
):
    tokens = q_buf.shape[0]
    padded = squares.shape[0]
    rows = dk // n_seq
    part = dk // PIECES
    seq = lax.axis_index("seq")
    last = n_seq - 1
    n_group = n_head * n_sub
    here = lax.axis_index("head") * n_sub + lax.axis_index("sub")

    barrier = pltpu.get_barrier_semaphore()
    for step in range(1, n_seq):
        pl.semaphore_signal(
            barrier, inc=1, device_id={"seq": lax.rem(seq + step, n_seq)}, device_id_type=MESH
        )
    for step in range(1, n_group):
        there = lax.rem(here + step, n_group)
        pl.semaphore_signal(
            barrier, inc=1,
            device_id={"head": there // n_sub, "sub": lax.rem(there, n_sub)},
            device_id_type=MESH,
        )

    def columns(h):
        return pl.ds(pl.multiple_of(h * dk, dk), dk)

    def load(h, slot):
        hbm, buf = ((k_hbm, k_buf), (v_hbm, v_buf), (q_hbm, q_buf))[slot]
        return pltpu.make_async_copy(hbm.at[:, columns(h)], buf.at[:, columns(h)], in_sem.at[slot, h])

    def store(h):
        return pltpu.make_async_copy(mix.at[:, columns(h)], mixed_hbm.at[:, columns(h)], out_sem.at[h])

    def piece(h, p):
        span = pl.ds(p * part, part)
        return pltpu.make_async_remote_copy(
            src_ref=outgoing.at[h, span], dst_ref=held.at[h, span],
            send_sem=send_sem.at[h, p], recv_sem=recv_sem.at[h, p],
            device_id={"seq": lax.rem(seq + 1, n_seq)}, device_id_type=MESH,
        )

    def start_loads(h, carry):
        for slot in range(3):
            load(h, slot).start()
        return carry

    lax.fori_loop(0, heads, start_loads, 0)

    @pl.when(seq == 0)
    def _():
        held[...] = jnp.zeros_like(held)

    squares[...] = jnp.zeros_like(squares)
    position = lax.broadcasted_iota(jnp.int32, (tokens, dk), 0).astype(F32)
    pl.semaphore_wait(barrier, n_seq - 1 + n_group - 1)

    def head_step(h, carry):
        cols = columns(h)
        rate = jnp.full((1, dk), exps[h], jnp.int32).astype(F32) / (8.0 * tokens * n_seq)
        load(h, 0).wait()
        load(h, 1).wait()
        scaled = (v_buf[:, cols].astype(F32) * jnp.exp2(position * rate)).astype(BF16)
        v_buf[:, cols] = scaled
        outgoing[h] = dot(k_buf[:, cols], scaled, ((0,), (0,))) * jnp.exp2(-rate * (tokens - 1.0))

        @pl.when(seq == 0)
        def _():
            for p in range(PIECES):
                piece(h, p).start()

        load(h, 2).wait()
        block = ROW_BLOCK if tokens % ROW_BLOCK == 0 else tokens
        lower = lax.broadcasted_iota(jnp.int32, (block, block), 0) >= lax.broadcasted_iota(
            jnp.int32, (block, block), 1
        )
        for top in range(0, tokens, block):
            q_rows = q_buf[top : top + block, cols]
            diagonal = dot(q_rows, k_buf[top : top + block, cols], ((1,), (1,)))
            weights = jnp.where(lower, diagonal, 0.0).astype(BF16)
            total = dot(weights, v_buf[top : top + block, cols], ((1,), (0,)))
            if top:
                before = dot(q_rows, k_buf[:top, cols], ((1,), (1,))).astype(BF16)
                total += dot(before, v_buf[:top, cols], ((1,), (0,)))
            mix[top : top + block, cols] = total

        block_decay = jnp.exp2(-rate * tokens)

        @pl.when(seq > 0)
        def _():
            for p in range(PIECES):
                span = pl.ds(p * part, part)
                piece(h, p).wait_recv()
                outgoing[h, span] = outgoing[h, span] + held[h, span] * block_decay

                @pl.when(seq < last)
                def _():
                    piece(h, p).start()

        @pl.when(seq == last)
        def _():
            for b in range(n_seq):
                final_rows[b, h] = outgoing[h, b * rows : (b + 1) * rows]
            for b in range(last):
                pltpu.make_async_remote_copy(
                    src_ref=final_rows.at[b, h], dst_ref=final_hbm.at[h],
                    send_sem=fin_send, recv_sem=fin_recv,
                    device_id={"seq": b}, device_id_type=MESH,
                ).start()

        state = (held[h] * jnp.exp2(-rate)).astype(BF16)
        inter = dot(q_buf[:, cols], state, ((1,), (0,)))
        mixed = (mix[:, cols] + inter) * jnp.exp2(-(position * rate))
        mix[:, cols] = mixed
        squares[:tokens] += mixed * mixed
        store(h).start()
        return carry

    lax.fori_loop(0, heads, head_step, 0)

    sums[here] = jnp.broadcast_to(
        jnp.sum(squares[...].T, axis=0, keepdims=True), (8, padded)
    )

    def sum_copy(step, slot, target):
        return pltpu.make_async_remote_copy(
            src_ref=sums.at[slot], dst_ref=sums.at[slot],
            send_sem=sum_send.at[step], recv_sem=sum_recv.at[step],
            device_id={"head": target // n_sub, "sub": lax.rem(target, n_sub)},
            device_id_type=MESH,
        )

    for step in range(1, n_group):
        sum_copy(step, here, lax.rem(here + step, n_group)).start()
    for step in range(1, n_group):
        source = lax.rem(here - step + n_group, n_group)
        sum_copy(step, source, source).wait_recv()
    total = sums[0]
    for slot in range(1, n_group):
        total += sums[slot]
    factor = lax.rsqrt(total / (heads * dk * n_group) + 1e-06)
    inv[...] = jnp.broadcast_to(factor[:1], (dk, padded)).T[:tokens]
    inv_copy = pltpu.make_async_copy(inv, inv_hbm, tail_sem.at[0])
    inv_copy.start()

    @pl.when(seq == last)
    def _():
        own = pltpu.make_async_copy(final_rows.at[last], final_hbm, tail_sem.at[1])
        own.start()
        sent = final_rows.at[pl.ds(0, last)]
        pltpu.make_async_copy(sent, sent, fin_send).wait()
        own.wait()

    @pl.when(seq < last)
    def _():
        pltpu.make_async_copy(final_hbm, final_hbm, fin_recv).wait()

        def finish(h, carry):
            for p in range(PIECES):
                piece(h, p).wait_send()
            return carry

        lax.fori_loop(0, heads, finish, 0)

    for step in range(1, n_group):
        sum_copy(step, here, lax.rem(here + step, n_group)).wait_send()

    def stored(h, carry):
        store(h).wait()
        return carry

    lax.fori_loop(0, heads, stored, 0)
    inv_copy.wait()


def local(n_seq, n_head, n_sub, queries, keys, values, decay_exp, gain):
    tokens, features = queries.shape
    heads = decay_exp.shape[0]
    dk = features // heads
    rows = dk // n_seq
    padded = -(-tokens // 128) * 128
    n_group = n_head * n_sub
    hbm = pl.BlockSpec(memory_space=pl.ANY)
    mixed, inv, final = pl.pallas_call(
        functools.partial(mix_kernel, n_seq, n_head, n_sub, heads, dk),
        out_shape=(
            jax.ShapeDtypeStruct((tokens, features), F32),
            jax.ShapeDtypeStruct((tokens, dk), F32),
            jax.ShapeDtypeStruct((heads, rows, dk), F32),
        ),
        in_specs=[pl.BlockSpec(memory_space=pltpu.SMEM)] + [pl.BlockSpec(memory_space=pltpu.HBM)] * 3,
        out_specs=(hbm, hbm, hbm),
        scratch_shapes=[
            pltpu.VMEM((tokens, features), BF16),
            pltpu.VMEM((tokens, features), BF16),
            pltpu.VMEM((tokens, features), BF16),
            pltpu.VMEM((tokens, features), F32),
            pltpu.VMEM((heads, dk, dk), F32),
            pltpu.VMEM((heads, dk, dk), F32),
            pltpu.VMEM((n_seq, heads, rows, dk), F32),
            pltpu.VMEM((padded, dk), F32),
            pltpu.VMEM((n_group, 8, padded), F32),
            pltpu.VMEM((tokens, dk), F32),
            pltpu.SemaphoreType.DMA((3, heads)),
            pltpu.SemaphoreType.DMA((heads,)),
            pltpu.SemaphoreType.DMA((heads, PIECES)),
            pltpu.SemaphoreType.DMA((heads, PIECES)),
            pltpu.SemaphoreType.DMA,
            pltpu.SemaphoreType.DMA,
            pltpu.SemaphoreType.DMA((n_group,)),
            pltpu.SemaphoreType.DMA((n_group,)),
            pltpu.SemaphoreType.DMA((2,)),
        ],
        compiler_params=pltpu.CompilerParams(
            collective_id=0, has_side_effects=True, vmem_limit_bytes=40 * 1024 * 1024
        ),
        name="mix",
    )(decay_exp, queries, keys, values)
    normed = (mixed * inv[:, :1] * gain[None, :]).astype(BF16)
    return normed, final


def solution(mesh):
    return jax.shard_map(
        functools.partial(local, mesh.shape["seq"], mesh.shape["head"], mesh.shape["sub"]),
        mesh=mesh,
        in_specs=(
            P(("groups", "seq"), ("head", "sub")),
            P(("groups", "seq"), ("head", "sub")),
            P(("groups", "seq"), ("head", "sub")),
            P(("head", "sub")),
            P(("head", "sub")),
        ),
        out_specs=(
            P(("groups", "seq"), ("head", "sub")),
            P(("groups", "head", "sub"), "seq", None),
        ),
        check_vma=False,
    )
```

time: 93.2 us -> 52.2 us (0.56)
  Pallas kernels: 0 us -> 42.9 us
  waiting for transfers between devices: 32.7 us -> 0 us
  matrix products: 31 us -> 0 us
  starting transfers between devices: 10.8 us -> 0 us
  other arithmetic: 7.7 us -> 1.86 us
  blocking collectives: 5.83 us -> 0 us
  local copies, waits for them, and re-layouts: 4.14 us -> 6.52 us
    pallas_call x0 -> x1, Pallas kernels: none -> 42.9 us  [local(): pl.pallas_call(functools.partial(mix_kernel, n_seq, n_head, n_sub, heads,...]
    all_to_all x2 -> x0, waiting for transfers between devices: 32.7 us -> none  [the longest x1 23.1 us: local(): lax.all_to_all(local_state[None], 'seq', split_axis=2, concat_axis=0, til...]
    dot_general x5 -> x0, matrix products: 31 us -> none  [the longest x1 12.4 us: local(): jnp.einsum('hij,jhd->ihd', weights, value_heads, preferred_element_type=j...]
    all_to_all x2 -> x0, starting transfers between devices: 10.8 us -> none  [the longest x1 6.35 us: local(): lax.all_to_all(local_state[None], 'seq', split_axis=2, concat_axis=0, til...]
    unnamed x4 -> x11, local copies, waits for them, and re-layouts: 0.02 us -> 6.35 us
    psum x1 -> x0, blocking collectives: 5.83 us -> none  [local(): summed = lax.psum(squares, ('head', 'sub'))]
    convert_element_type x3 -> x1, other arithmetic: 4.22 us -> 1.86 us  [local(): normed = (mixed * inv[:, :1] * gain[None, :]).astype(BF16)]
    broadcast_in_dim x1 -> x0, local copies, waits for them, and re-layouts: 1.58 us -> none  [local(): local_state[None]]
  transfers between devices with their start and end apart: 2 -> 0, of which waited for: 2 -> 0; matrix products, arithmetic and copies ran while one was open for 20% -> 0% of each run, Pallas kernels for 0% -> 0%
where the time goes in v1:
time: 52.2 us; the launch traced here: 52 us
  Pallas kernels  42.9 us (82%)
  local copies, waits for them, and re-layouts  6.52 us (12%)
  other arithmetic  1.86 us (4%)
  between operations  0.66 us (1%)
    pallas_call x1, Pallas kernels, local(): pl.pallas_call(functools.partial(mix_kernel, n_seq, n_head, n_sub, heads,...  42.9 us
    unnamed x11, local copies, waits for them, and re-layouts  6.35 us
    convert_element_type x1, other arithmetic, local(): normed = (mixed * inv[:, :1] * gain[None, :]).astype(BF16)  1.86 us

profile of v1, /device:TPU:0, one launch (start us, length us, event | category | flops | bytes accessed | tf_op | source)
XLA Modules:
  0.0 52.0 jit_solution(11807771201968105234)
XLA Ops:
  0.6 0.0 copy-start
  0.6 1.7 %copy-done = bf16[576,2048]{1,0:T(8,128)(2,1)S(1)} copy-done((bf16[576,2048]{1,0:T(8,128)(2,1)S(1)}, bf16[576,2048]{1,0:T(8,128)(2,1)}, u32[]{:S(2)}) %copy-start) | copy-done | bytes 2359320
  2.3 0.0 copy-start.1
  2.3 1.7 %copy-done.1 = bf16[576,2048]{1,0:T(8,128)(2,1)S(1)} copy-done((bf16[576,2048]{1,0:T(8,128)(2,1)S(1)}, bf16[576,2048]{1,0:T(8,128)(2,1)}, u32[]{:S(2)}) %copy-start.1) | copy-done | bytes 2359320
  4.0 0.0 copy-start.2
  4.0 1.7 %copy-done.2 = bf16[576,2048]{1,0:T(8,128)(2,1)S(1)} copy-done((bf16[576,2048]{1,0:T(8,128)(2,1)S(1)}, bf16[576,2048]{1,0:T(8,128)(2,1)}, u32[]{:S(2)}) %copy-start.2) | copy-done | bytes 2359320
  5.6 0.0 copy-start.3
  5.6 0.7 %copy-done.3 = s32[16]{0:T(128)S(1)} copy-done((s32[16]{0:T(128)S(1)}, s32[16]{0:T(128)}, u32[]{:S(2)}) %copy-start.3) | copy-done | bytes 88
  6.3 0.0 copy-start.4
  6.3 42.9 %mix.1 = (f32[576,2048]{1,0:T(8,128)S(1)}, f32[576,128]{1,0:T(8,128)S(1)}, f32[16,32,128]{2,1,0:T(8,128)S(1)}) custom-call(s32[16]{0:T(128)S(1)} %copy-done.3, bf16[576,2048]{1,0:T(8,128)(2,1)S(1)} %copy-done, bf16[576,2048]{1,0:T(8,128)(2,1)S(1)} %copy-done.1, bf16[576,2048]{1,0:T(8,128)(2,1)S(1)} %copy-done.2), custom_call_target="tpu_custom_call" | custom-call | tf_op jit(solution)/shard_map/mix/pallas_call | solution.py:209
  49.2 0.2 slice_reduce_fusion
  49.4 0.0 copy-done.4
  49.4 1.9 %multiply_convert_fusion = bf16[576,2048]{1,0:T(8,128)(2,1)} fusion(f32[576,2048]{1,0:T(8,128)S(1)} %get-tuple-element.5, f32[2048]{0:T(1024)S(1)} %copy-done.4, f32[576]{0:T(1024)S(1)} %slice_reduce_fusion), kind=kLoop, calls=%fused_computation | loop fusion | flops 3538944 | bytes 7088384 | tf_op jit(solution)/shard_map/convert_element_type | solution.py:244
  51.3 0.7 %copy.8 = f32[16,32,128]{2,1,0:T(8,128)} copy(f32[16,32,128]{2,1,0:T(8,128)S(1)} %get-tuple-element.11) | data formatting | bytes 524288
Async XLA Ops:
  0.6 1.7 %copy-start = (bf16[576,2048]{1,0:T(8,128)(2,1)S(1)}, bf16[576,2048]{1,0:T(8,128)(2,1)}, u32[]{:S(2)}) copy-start(bf16[576,2048]{1,0:T(8,128)(2,1)} %q_hbm.1) | copy-start | bytes 7077892
  2.3 1.7 %copy-start.1 = (bf16[576,2048]{1,0:T(8,128)(2,1)S(1)}, bf16[576,2048]{1,0:T(8,128)(2,1)}, u32[]{:S(2)}) copy-start(bf16[576,2048]{1,0:T(8,128)(2,1)} %k_hbm.1) | copy-start | bytes 7077892
  4.0 1.7 %copy-start.2 = (bf16[576,2048]{1,0:T(8,128)(2,1)S(1)}, bf16[576,2048]{1,0:T(8,128)(2,1)}, u32[]{:S(2)}) copy-start(bf16[576,2048]{1,0:T(8,128)(2,1)} %v_hbm.1) | copy-start | bytes 7077892
  5.6 0.7 %copy-start.3 = (s32[16]{0:T(128)S(1)}, s32[16]{0:T(128)}, u32[]{:S(2)}) copy-start(s32[16]{0:T(128)} %exps.1) | copy-start | bytes 196
  6.3 43.1 %copy-start.4 = (f32[2048]{0:T(1024)S(1)}, f32[2048]{0:T(1024)}, u32[]{:S(2)}) copy-start(f32[2048]{0:T(1024)} %param.9) | copy-start | bytes 24580

commit v2 on v1

--- a/solution.py
+++ b/solution.py
@@ -22,7 +22,7 @@
     n_seq, n_head, n_sub, heads, dk,
     exps, q_hbm, k_hbm, v_hbm,
     mixed_hbm, inv_hbm, final_hbm,
-    q_buf, k_buf, v_buf, mix, held, outgoing, final_rows, squares, sums, inv,
+    q_buf, k_buf, v_buf, mix, held, outgoing, final_rows, squares, sums, inv, running, late, final,
     in_sem, out_sem, send_sem, recv_sem, fin_send, fin_recv, sum_send, sum_recv, tail_sem,
 ):
     tokens = q_buf.shape[0]
@@ -85,29 +85,44 @@
         rate = jnp.full((1, dk), exps[h], jnp.int32).astype(F32) / (8.0 * tokens * n_seq)
         load(h, 0).wait()
         load(h, 1).wait()
-        scaled = (v_buf[:, cols].astype(F32) * jnp.exp2(position * rate)).astype(BF16)
-        v_buf[:, cols] = scaled
-        outgoing[h] = dot(k_buf[:, cols], scaled, ((0,), (0,))) * jnp.exp2(-rate * (tokens - 1.0))
+        block = ROW_BLOCK if tokens % ROW_BLOCK == 0 else tokens
+        tops = range(0, tokens, block)
+        state = jnp.zeros((dk, dk), F32)
+        for c, top in enumerate(tops):
+            span = slice(top, top + block)
+            scaled = (v_buf[span, cols].astype(F32) * jnp.exp2(position[span] * rate)).astype(BF16)
+            v_buf[span, cols] = scaled
+            running[c] = state
+            state += dot(k_buf[span, cols], scaled, ((0,), (0,)))
+        own = state * jnp.exp2(-rate * (tokens - 1.0))
+        outgoing[h] = own
+        for b in range(n_seq):
+            final_rows[b, h] = own[b * rows : (b + 1) * rows]
 
         @pl.when(seq == 0)
         def _():
             for p in range(PIECES):
                 piece(h, p).start()
 
+        for b in range(last):
+
+            @pl.when(b < seq)
+            def _():
+                pltpu.make_async_remote_copy(
+                    src_ref=final_rows.at[b, h], dst_ref=late.at[seq, h],
+                    send_sem=fin_send.at[b], recv_sem=fin_recv.at[seq],
+                    device_id={"seq": b}, device_id_type=MESH,
+                ).start()
+
         load(h, 2).wait()
-        block = ROW_BLOCK if tokens % ROW_BLOCK == 0 else tokens
         lower = lax.broadcasted_iota(jnp.int32, (block, block), 0) >= lax.broadcasted_iota(
             jnp.int32, (block, block), 1
         )
-        for top in range(0, tokens, block):
-            q_rows = q_buf[top : top + block, cols]
-            diagonal = dot(q_rows, k_buf[top : top + block, cols], ((1,), (1,)))
-            weights = jnp.where(lower, diagonal, 0.0).astype(BF16)
-            total = dot(weights, v_buf[top : top + block, cols], ((1,), (0,)))
-            if top:
-                before = dot(q_rows, k_buf[:top, cols], ((1,), (1,))).astype(BF16)
-                total += dot(before, v_buf[:top, cols], ((1,), (0,)))
-            mix[top : top + block, cols] = total
+        for top in tops:
+            span = slice(top, top + block)
+            scores = dot(q_buf[span, cols], k_buf[span, cols], ((1,), (1,)))
+            weights = jnp.where(lower, scores, 0.0).astype(BF16)
+            mix[span, cols] = dot(weights, v_buf[span, cols], ((1,), (0,)))
 
         block_decay = jnp.exp2(-rate * tokens)
 
@@ -116,28 +131,19 @@
             for p in range(PIECES):
                 span = pl.ds(p * part, part)
                 piece(h, p).wait_recv()
-                outgoing[h, span] = outgoing[h, span] + held[h, span] * block_decay
 
                 @pl.when(seq < last)
                 def _():
+                    outgoing[h, span] = outgoing[h, span] + held[h, span] * block_decay
                     piece(h, p).start()
 
-        @pl.when(seq == last)
-        def _():
-            for b in range(n_seq):
-                final_rows[b, h] = outgoing[h, b * rows : (b + 1) * rows]
-            for b in range(last):
-                pltpu.make_async_remote_copy(
-                    src_ref=final_rows.at[b, h], dst_ref=final_hbm.at[h],
-                    send_sem=fin_send, recv_sem=fin_recv,
-                    device_id={"seq": b}, device_id_type=MESH,
-                ).start()
-
-        state = (held[h] * jnp.exp2(-rate)).astype(BF16)
-        inter = dot(q_buf[:, cols], state, ((1,), (0,)))
-        mixed = (mix[:, cols] + inter) * jnp.exp2(-(position * rate))
-        mix[:, cols] = mixed
-        squares[:tokens] += mixed * mixed
+        start = held[h] * jnp.exp2(-rate)
+        for c, top in enumerate(tops):
+            span = slice(top, top + block)
+            inter = dot(q_buf[span, cols], (start + running[c]).astype(BF16), ((1,), (0,)))
+            mixed = (mix[span, cols] + inter) * jnp.exp2(-(position[span] * rate))
+            mix[span, cols] = mixed
+            squares[span] += mixed * mixed
         store(h).start()
         return carry
 
@@ -157,6 +163,26 @@
 
     for step in range(1, n_group):
         sum_copy(step, here, lax.rem(here + step, n_group)).start()
+    for b in range(n_seq):
+
+        @pl.when(seq == b)
+        def _():
+            for m in range(b + 1, n_seq):
+                pltpu.make_async_copy(late.at[m], late.at[m], fin_recv.at[m]).wait()
+
+            def finals(h, carry):
+                rate = jnp.full((1, dk), exps[h], jnp.int32).astype(F32) / (8.0 * n_seq)
+                total = held[h, b * rows : (b + 1) * rows] * jnp.exp2(-rate * (n_seq - b))
+                total += final_rows[b, h] * jnp.exp2(-rate * (last - b))
+                for m in range(b + 1, n_seq):
+                    total += late[m, h] * jnp.exp2(-rate * (last - m))
+                final[h] = total
+                return carry
+
+            lax.fori_loop(0, heads, finals, 0)
+
+    final_copy = pltpu.make_async_copy(final, final_hbm, tail_sem.at[1])
+    final_copy.start()
     for step in range(1, n_group):
         source = lax.rem(here - step + n_group, n_group)
         sum_copy(step, source, source).wait_recv()
@@ -168,18 +194,14 @@
     inv_copy = pltpu.make_async_copy(inv, inv_hbm, tail_sem.at[0])
     inv_copy.start()
 
-    @pl.when(seq == last)
-    def _():
-        own = pltpu.make_async_copy(final_rows.at[last], final_hbm, tail_sem.at[1])
-        own.start()
-        sent = final_rows.at[pl.ds(0, last)]
-        pltpu.make_async_copy(sent, sent, fin_send).wait()
-        own.wait()
+    for b in range(last):
+
+        @pl.when(b < seq)
+        def _():
+            pltpu.make_async_copy(final_rows.at[b], final_rows.at[b], fin_send.at[b]).wait()
 
     @pl.when(seq < last)
     def _():
-        pltpu.make_async_copy(final_hbm, final_hbm, fin_recv).wait()
-
         def finish(h, carry):
             for p in range(PIECES):
                 piece(h, p).wait_send()
@@ -196,6 +218,7 @@
 
     lax.fori_loop(0, heads, stored, 0)
     inv_copy.wait()
+    final_copy.wait()
 
 
 def local(n_seq, n_head, n_sub, queries, keys, values, decay_exp, gain):
@@ -226,12 +249,15 @@
             pltpu.VMEM((padded, dk), F32),
             pltpu.VMEM((n_group, 8, padded), F32),
             pltpu.VMEM((tokens, dk), F32),
+            pltpu.VMEM((max(1, tokens // ROW_BLOCK), dk, dk), F32),
+            pltpu.VMEM((n_seq, heads, rows, dk), F32),
+            pltpu.VMEM((heads, rows, dk), F32),
             pltpu.SemaphoreType.DMA((3, heads)),
             pltpu.SemaphoreType.DMA((heads,)),
             pltpu.SemaphoreType.DMA((heads, PIECES)),
             pltpu.SemaphoreType.DMA((heads, PIECES)),
-            pltpu.SemaphoreType.DMA,
-            pltpu.SemaphoreType.DMA,
+            pltpu.SemaphoreType.DMA((n_seq,)),
+            pltpu.SemaphoreType.DMA((n_seq,)),
             pltpu.SemaphoreType.DMA((n_group,)),
             pltpu.SemaphoreType.DMA((n_group,)),
             pltpu.SemaphoreType.DMA((2,)),
@@ -240,7 +266,7 @@
             collective_id=0, has_side_effects=True, vmem_limit_bytes=40 * 1024 * 1024
         ),
         name="mix",
-    )(decay_exp, queries, keys, values)
+    )(decay_exp, *(pltpu.with_memory_space_constraint(x, pltpu.HBM) for x in (queries, keys, values)))
     normed = (mixed * inv[:, :1] * gain[None, :]).astype(BF16)
     return normed, final
 

time: 52.2 us -> 46.3 us (0.89)
  local copies, waits for them, and re-layouts: 6.52 us -> 1.52 us
  Pallas kernels: 42.9 us -> 42.1 us
    unnamed x11 -> x5, local copies, waits for them, and re-layouts: 6.35 us -> 1.35 us
    pallas_call x1, Pallas kernels: 42.9 us -> 42.1 us  [local(): pl.pallas_call(functools.partial(mix_kernel, n_seq, n_head, n_sub, heads,...]
where the time goes in v2:
time: 46.3 us; the launch traced here: 46.2 us
  Pallas kernels  42.1 us (91%)
  other arithmetic  1.86 us (4%)
  local copies, waits for them, and re-layouts  1.52 us (3%)
  between operations  0.66 us (1%)
    pallas_call x1, Pallas kernels, local(): pl.pallas_call(functools.partial(mix_kernel, n_seq, n_head, n_sub, heads,...  42.1 us
    convert_element_type x1, other arithmetic, local(): normed = (mixed * inv[:, :1] * gain[None, :]).astype(BF16)  1.86 us
    unnamed x5, local copies, waits for them, and re-layouts  1.35 us

profile of v2, /device:TPU:0, one launch (start us, length us, event | category | flops | bytes accessed | tf_op | source)
XLA Modules:
  0.0 46.2 jit_solution(7187717408169046534)
XLA Ops:
  0.6 0.0 copy-start
  0.6 0.6 %copy-done = s32[16]{0:T(128)S(1)} copy-done((s32[16]{0:T(128)S(1)}, s32[16]{0:T(128)}, u32[]{:S(2)}) %copy-start) | copy-done | bytes 88
  1.3 0.0 copy-start.1
  1.3 42.1 %mix.1 = (f32[576,2048]{1,0:T(8,128)S(1)}, f32[576,128]{1,0:T(8,128)S(1)}, f32[16,32,128]{2,1,0:T(8,128)S(1)}) custom-call(s32[16]{0:T(128)S(1)} %copy-done, bf16[576,2048]{1,0:T(8,128)(2,1)} %q_hbm.1, bf16[576,2048]{1,0:T(8,128)(2,1)} %k_hbm.1, bf16[576,2048]{1,0:T(8,128)(2,1)} %v_hbm.1), custom_call_target="tpu_custom_call" | custom-call | tf_op jit(solution)/shard_map/mix/pallas_call | solution.py:232
  43.4 0.2 slice_reduce_fusion
  43.6 0.0 copy-done.1
  43.6 1.9 %multiply_convert_fusion = bf16[576,2048]{1,0:T(8,128)(2,1)} fusion(f32[576,2048]{1,0:T(8,128)S(1)} %get-tuple-element.5, f32[2048]{0:T(1024)S(1)} %copy-done.1, f32[576]{0:T(1024)S(1)} %slice_reduce_fusion), kind=kLoop, calls=%fused_computation | loop fusion | flops 3538944 | bytes 7088384 | tf_op jit(solution)/shard_map/convert_element_type | solution.py:270
  45.5 0.7 %copy.8 = f32[16,32,128]{2,1,0:T(8,128)} copy(f32[16,32,128]{2,1,0:T(8,128)S(1)} %get-tuple-element.11) | data formatting | bytes 524288
Async XLA Ops:
  0.6 0.7 %copy-start = (s32[16]{0:T(128)S(1)}, s32[16]{0:T(128)}, u32[]{:S(2)}) copy-start(s32[16]{0:T(128)} %exps.1) | copy-start | bytes 196
  1.3 42.3 %copy-start.1 = (f32[2048]{0:T(1024)S(1)}, f32[2048]{0:T(1024)}, u32[]{:S(2)}) copy-start(f32[2048]{0:T(1024)} %param.9) | copy-start | bytes 24580

commit v3 on v2

--- a/solution.py
+++ b/solution.py
@@ -11,6 +11,8 @@
 F32 = jnp.float32
 BF16 = jnp.bfloat16
 PIECES = 2
+NORM_VMEM = 16
+LEAD = 3
 ROW_BLOCK = 192
 
 
@@ -80,19 +82,20 @@
     position = lax.broadcasted_iota(jnp.int32, (tokens, dk), 0).astype(F32)
     pl.semaphore_wait(barrier, n_seq - 1 + n_group - 1)
 
-    def head_step(h, carry):
+    block = ROW_BLOCK if tokens % ROW_BLOCK == 0 else tokens
+    tops = range(0, tokens, block)
+
+    def prepare(h, carry):
         cols = columns(h)
         rate = jnp.full((1, dk), exps[h], jnp.int32).astype(F32) / (8.0 * tokens * n_seq)
         load(h, 0).wait()
         load(h, 1).wait()
-        block = ROW_BLOCK if tokens % ROW_BLOCK == 0 else tokens
-        tops = range(0, tokens, block)
         state = jnp.zeros((dk, dk), F32)
         for c, top in enumerate(tops):
             span = slice(top, top + block)
             scaled = (v_buf[span, cols].astype(F32) * jnp.exp2(position[span] * rate)).astype(BF16)
             v_buf[span, cols] = scaled
-            running[c] = state
+            running[h, c] = state
             state += dot(k_buf[span, cols], scaled, ((0,), (0,)))
         own = state * jnp.exp2(-rate * (tokens - 1.0))
         outgoing[h] = own
@@ -123,7 +126,11 @@
             scores = dot(q_buf[span, cols], k_buf[span, cols], ((1,), (1,)))
             weights = jnp.where(lower, scores, 0.0).astype(BF16)
             mix[span, cols] = dot(weights, v_buf[span, cols], ((1,), (0,)))
-
+        return carry
+
+    def head_step(h, carry):
+        cols = columns(h)
+        rate = jnp.full((1, dk), exps[h], jnp.int32).astype(F32) / (8.0 * tokens * n_seq)
         block_decay = jnp.exp2(-rate * tokens)
 
         @pl.when(seq > 0)
@@ -140,13 +147,20 @@
         start = held[h] * jnp.exp2(-rate)
         for c, top in enumerate(tops):
             span = slice(top, top + block)
-            inter = dot(q_buf[span, cols], (start + running[c]).astype(BF16), ((1,), (0,)))
+            inter = dot(q_buf[span, cols], (start + running[h, c]).astype(BF16), ((1,), (0,)))
             mixed = (mix[span, cols] + inter) * jnp.exp2(-(position[span] * rate))
             mix[span, cols] = mixed
             squares[span] += mixed * mixed
         store(h).start()
-        return carry
-
+
+        @pl.when(h + lead < heads)
+        def _():
+            prepare(h + lead, 0)
+
+        return carry
+
+    lead = jnp.minimum(1 + LEAD * seq, heads)
+    lax.fori_loop(0, lead, prepare, 0)
     lax.fori_loop(0, heads, head_step, 0)
 
     sums[here] = jnp.broadcast_to(
@@ -218,6 +232,31 @@
 
     lax.fori_loop(0, heads, stored, 0)
     inv_copy.wait()
+    final_copy.wait()
+
+
+def norm_kernel(heads, dk, mixed, inv, final, gain, normed_hbm, final_hbm, normed, sems):
+    final_copy = pltpu.make_async_copy(final, final_hbm, sems.at[heads])
+    final_copy.start()
+
+    def columns(h):
+        return pl.ds(pl.multiple_of(h * dk, dk), dk)
+
+    def copy(h):
+        return pltpu.make_async_copy(normed.at[:, columns(h)], normed_hbm.at[:, columns(h)], sems.at[h])
+
+    def scale(h, carry):
+        cols = columns(h)
+        normed[:, cols] = (mixed[:, cols] * inv[...] * gain[:, cols]).astype(BF16)
+        copy(h).start()
+        return carry
+
+    def finish(h, carry):
+        copy(h).wait()
+        return carry
+
+    lax.fori_loop(0, heads, scale, 0)
+    lax.fori_loop(0, heads, finish, 0)
     final_copy.wait()
 
 
@@ -249,7 +288,7 @@
             pltpu.VMEM((padded, dk), F32),
             pltpu.VMEM((n_group, 8, padded), F32),
             pltpu.VMEM((tokens, dk), F32),
-            pltpu.VMEM((max(1, tokens // ROW_BLOCK), dk, dk), F32),
+            pltpu.VMEM((heads, max(1, tokens // ROW_BLOCK), dk, dk), F32),
             pltpu.VMEM((n_seq, heads, rows, dk), F32),
             pltpu.VMEM((heads, rows, dk), F32),
             pltpu.SemaphoreType.DMA((3, heads)),
@@ -266,9 +305,26 @@
             collective_id=0, has_side_effects=True, vmem_limit_bytes=40 * 1024 * 1024
         ),
         name="mix",
-    )(decay_exp, *(pltpu.with_memory_space_constraint(x, pltpu.HBM) for x in (queries, keys, values)))
-    normed = (mixed * inv[:, :1] * gain[None, :]).astype(BF16)
-    return normed, final
+    )(*(pltpu.with_memory_space_constraint(x, pltpu.HBM) for x in (decay_exp, queries, keys, values)))
+    vmem = pl.BlockSpec(memory_space=pltpu.VMEM)
+    return pl.pallas_call(
+        functools.partial(norm_kernel, heads, dk),
+        out_shape=(
+            jax.ShapeDtypeStruct((tokens, features), BF16),
+            jax.ShapeDtypeStruct((heads, rows, dk), F32),
+        ),
+        in_specs=[vmem] * 4,
+        out_specs=(pl.BlockSpec(memory_space=pltpu.HBM),) * 2,
+        scratch_shapes=[
+            pltpu.VMEM((tokens, features), BF16),
+            pltpu.SemaphoreType.DMA((heads + 1,)),
+        ],
+        compiler_params=pltpu.CompilerParams(vmem_limit_bytes=NORM_VMEM * 1024 * 1024),
+        name="norm",
+    )(
+        *(pltpu.with_memory_space_constraint(x, pltpu.VMEM) for x in (mixed, inv, final)),
+        gain.reshape(1, features),
+    )
 
 
 def solution(mesh):

time: 46.3 us -> 41.4 us (0.89)
  the two profiles are of different devices: /device:TPU:0 before, /device:TPU:25 now
where the time goes in v3:
time: 41.4 us; the launch traced here: 41.3 us
  Pallas kernels  40.6 us (98%)
  between operations  0.65 us (2%)
    pallas_call x1, Pallas kernels, local(): pl.pallas_call(functools.partial(mix_kernel, n_seq, n_head, n_sub, heads,...  38.8 us
    pallas_call x1, Pallas kernels, local(): pl.pallas_call(functools.partial(norm_kernel, heads, dk), out_shape=(jax....  1.79 us

profile of v3, /device:TPU:25, one launch (start us, length us, event | category | flops | bytes accessed | tf_op | source)
XLA Modules:
  0.0 41.3 jit_solution(15785195916500776625)
XLA Ops:
  0.6 0.0 copy-start
  0.6 38.8 %mix.1 = (f32[576,2048]{1,0:T(8,128)S(1)}, f32[576,128]{1,0:T(8,128)S(1)}, f32[16,32,128]{2,1,0:T(8,128)S(1)}) custom-call(s32[16]{0:T(128)} %exps.1, bf16[576,2048]{1,0:T(8,128)(2,1)} %q_hbm.1, bf16[576,2048]{1,0:T(8,128)(2,1)} %k_hbm.1, bf16[576,2048]{1,0:T(8,128)(2,1)} %v_hbm.1), custom_call_target="tpu_custom_call" | custom-call | tf_op jit(solution)/shard_map/mix/pallas_call | solution.py:271
  39.5 0.0 copy-done
  39.5 1.8 %norm.1 = (bf16[576,2048]{1,0:T(8,128)(2,1)}, f32[16,32,128]{2,1,0:T(8,128)}) custom-call(f32[576,2048]{1,0:T(8,128)S(1)} %get-tuple-element.5.mixed, f32[576,128]{1,0:T(8,128)S(1)} %get-tuple-element.6.inv, f32[16,32,128]{2,1,0:T(8,128)S(1)} %get-tuple-element.7.final, f32[1,2048]{1,0:T(1,128)S(1)} %bitcast.1), custom_call_target="tpu_custom_call" | custom-call | tf_op jit(solution)/shard_map/norm/pallas_call | solution.py:310
Async XLA Ops:
  0.6 38.9 %copy-start = (f32[2048]{0:T(1024)S(1)}, f32[2048]{0:T(1024)}, u32[]{:S(2)}) copy-start(f32[2048]{0:T(1024)} %param.9) | copy-start | bytes 24580

commit v4 on v3

--- a/solution.py
+++ b/solution.py
@@ -11,6 +11,7 @@
 F32 = jnp.float32
 BF16 = jnp.bfloat16
 PIECES = 2
+NORM_ROWS = 96
 NORM_VMEM = 16
 LEAD = 3
 ROW_BLOCK = 192
@@ -80,12 +81,11 @@
 
     squares[...] = jnp.zeros_like(squares)
     position = lax.broadcasted_iota(jnp.int32, (tokens, dk), 0).astype(F32)
-    pl.semaphore_wait(barrier, n_seq - 1 + n_group - 1)
 
     block = ROW_BLOCK if tokens % ROW_BLOCK == 0 else tokens
     tops = range(0, tokens, block)
 
-    def prepare(h, carry):
+    def prepare(h, carry, first=False):
         cols = columns(h)
         rate = jnp.full((1, dk), exps[h], jnp.int32).astype(F32) / (8.0 * tokens * n_seq)
         load(h, 0).wait()
@@ -101,6 +101,8 @@
         outgoing[h] = own
         for b in range(n_seq):
             final_rows[b, h] = own[b * rows : (b + 1) * rows]
+        if first:
+            pl.semaphore_wait(barrier, n_seq - 1 + n_group - 1)
 
         @pl.when(seq == 0)
         def _():
@@ -160,7 +162,8 @@
         return carry
 
     lead = jnp.minimum(1 + LEAD * seq, heads)
-    lax.fori_loop(0, lead, prepare, 0)
+    prepare(0, 0, first=True)
+    lax.fori_loop(1, lead, prepare, 0)
     lax.fori_loop(0, heads, head_step, 0)
 
     sums[here] = jnp.broadcast_to(
@@ -236,27 +239,25 @@
 
 
 def norm_kernel(heads, dk, mixed, inv, final, gain, normed_hbm, final_hbm, normed, sems):
-    final_copy = pltpu.make_async_copy(final, final_hbm, sems.at[heads])
+    final_copy = pltpu.make_async_copy(final, final_hbm, sems.at[mixed.shape[0] // NORM_ROWS + 1])
     final_copy.start()
 
-    def columns(h):
-        return pl.ds(pl.multiple_of(h * dk, dk), dk)
-
-    def copy(h):
-        return pltpu.make_async_copy(normed.at[:, columns(h)], normed_hbm.at[:, columns(h)], sems.at[h])
-
-    def scale(h, carry):
-        cols = columns(h)
-        normed[:, cols] = (mixed[:, cols] * inv[...] * gain[:, cols]).astype(BF16)
-        copy(h).start()
-        return carry
-
-    def finish(h, carry):
-        copy(h).wait()
-        return carry
-
-    lax.fori_loop(0, heads, scale, 0)
-    lax.fori_loop(0, heads, finish, 0)
+    tokens = mixed.shape[0]
+    block = NORM_ROWS if tokens % NORM_ROWS == 0 else tokens
+
+    def copy(n):
+        span = pl.ds(n * block, block)
+        return pltpu.make_async_copy(normed.at[span], normed_hbm.at[span], sems.at[n])
+
+    for n in range(tokens // block):
+        span = slice(n * block, (n + 1) * block)
+        scale = inv[span]
+        for h in range(heads):
+            cols = slice(h * dk, (h + 1) * dk)
+            normed[span, cols] = (mixed[span, cols] * scale * gain[:, cols]).astype(BF16)
+        copy(n).start()
+    for n in range(tokens // block):
+        copy(n).wait()
     final_copy.wait()
 
 
@@ -317,7 +318,7 @@
         out_specs=(pl.BlockSpec(memory_space=pltpu.HBM),) * 2,
         scratch_shapes=[
             pltpu.VMEM((tokens, features), BF16),
-            pltpu.SemaphoreType.DMA((heads + 1,)),
+            pltpu.SemaphoreType.DMA((tokens // NORM_ROWS + 2,)),
         ],
         compiler_params=pltpu.CompilerParams(vmem_limit_bytes=NORM_VMEM * 1024 * 1024),
         name="norm",

time: 41.4 us -> 40.9 us (0.988)
  Pallas kernels: 40.6 us -> 40.1 us
where the time goes in v4:
time: 40.9 us; the launch traced here: 40.7 us
  Pallas kernels  40.1 us (98%)
  between operations  0.65 us (2%)
    pallas_call x1, Pallas kernels, local(): pl.pallas_call(functools.partial(mix_kernel, n_seq, n_head, n_sub, heads,...  38.5 us
    pallas_call x1, Pallas kernels, local(): pl.pallas_call(functools.partial(norm_kernel, heads, dk), out_shape=(jax....  1.57 us

profile of v4, /device:TPU:25, one launch (start us, length us, event | category | flops | bytes accessed | tf_op | source)
XLA Modules:
  0.0 40.7 jit_solution(11375289037996872405)
XLA Ops:
  0.6 0.0 copy-start
  0.6 38.5 %mix.1 = (f32[576,2048]{1,0:T(8,128)S(1)}, f32[576,128]{1,0:T(8,128)S(1)}, f32[16,32,128]{2,1,0:T(8,128)S(1)}) custom-call(s32[16]{0:T(128)} %exps.1, bf16[576,2048]{1,0:T(8,128)(2,1)} %q_hbm.1, bf16[576,2048]{1,0:T(8,128)(2,1)} %k_hbm.1, bf16[576,2048]{1,0:T(8,128)(2,1)} %v_hbm.1), custom_call_target="tpu_custom_call" | custom-call | tf_op jit(solution)/shard_map/mix/pallas_call | solution.py:272
  39.2 0.0 copy-done
  39.2 1.6 %norm.1 = (bf16[576,2048]{1,0:T(8,128)(2,1)}, f32[16,32,128]{2,1,0:T(8,128)}) custom-call(f32[576,2048]{1,0:T(8,128)S(1)} %get-tuple-element.5.mixed, f32[576,128]{1,0:T(8,128)S(1)} %get-tuple-element.6.inv, f32[16,32,128]{2,1,0:T(8,128)S(1)} %get-tuple-element.7.final, f32[1,2048]{1,0:T(1,128)S(1)} %bitcast.1), custom_call_target="tpu_custom_call" | custom-call | tf_op jit(solution)/shard_map/norm/pallas_call | solution.py:311
Async XLA Ops:
  0.6 38.5 %copy-start = (f32[2048]{0:T(1024)S(1)}, f32[2048]{0:T(1024)}, u32[]{:S(2)}) copy-start(f32[2048]{0:T(1024)} %param.9) | copy-start | bytes 24580
